TPU v7x, 128 devices: a whole 4x4x4 slice. The times are simulated.
128 devices in a mesh: row: 4 (over y), col: 32 (over x, z, core).
Axes of the slice: x: 4, y: 4, z: 4, core: 2. Of those that a mesh axis runs over, the one named last changes fastest.
Arguments:
- coordinates: float32 [3, 65536], replicated, may hold values from 0 to 1
- ordering: int32 [65536], replicated, may hold values from 0 to 65535, each once
- neighbours: int32 [256, 4], replicated, may hold values from 0 to 254, as said below
- cross: float32 [256, 4, 256, 256], P(('row', 'col')), may hold values from -0.1875 to 0.1875
- whitening: float32 [256, 256, 256], P(('row', 'col')), may hold values from -0.1875 to 0.1875
- solution: float32 [256, 8, 256], P(('row', 'col')), may hold values from -6 to 6
- residual: float32 [256, 8, 256], P(('row', 'col')), may hold values from -40 to 40
- direction: float32 [256, 8, 256], P(('row', 'col')), may hold values from -40 to 40
Outputs:
- solution_next: float32 [256, 8, 256], P(('row', 'col'))
- residual_next: float32 [256, 8, 256], P(('row', 'col'))
- direction_next: float32 [256, 8, 256], P(('row', 'col'))
Inputs may be any that keep to these rules, and one draw needn't show every extreme that they name: `neighbours`: row b lists b - 1 first, then further distinct blocks below b - 1; where fewer than 4 earlier blocks exist the remaining entries equal b itself.
All inputs are finite; a program needn't handle non-finite values.
Results may differ from a plain program's by a relative error of at most 0.00023.
Values sent between devices are 32-bit elements; how exact they have to be, the bound alone decides.
No kernel may reach another device: no remote copies, remote signals or barrier semaphores. Data moves between devices by JAX's collectives and lax.ppermute only.
A program may use at most 192 MiB of HBM per device.

v0:
```python
import math
import jax
import jax.numpy as jnp
from jax import lax
from jax.sharding import PartitionSpec as P

kernel_rate = math.sqrt(3.0) / 0.3
variance = 0.05
nugget = 1.0
highest = lax.Precision.HIGHEST


def covariance(rows, columns):
    apart_x = rows[0][:, None] - columns[0][None, :]
    apart_y = rows[1][:, None] - columns[1][None, :]
    apart_z = rows[2][:, None] - columns[2][None, :]
    distance = jnp.sqrt(apart_x * apart_x + apart_y * apart_y + apart_z * apart_z)
    scaled = kernel_rate * distance
    return variance * (1.0 + scaled) * jnp.exp(-scaled)


def per_device(coordinates, ordering, neighbours, cross, whitening, solution, residual, direction):
    own_blocks = residual.shape[0]
    rhs_count = residual.shape[1]
    block_size = residual.shape[2]
    total_blocks = ordering.shape[0] // block_size
    points = coordinates[:, ordering].reshape(3, total_blocks, block_size)
    device = lax.axis_index(("row", "col"))
    first_block = device * own_blocks
    own_ids = first_block + jnp.arange(own_blocks, dtype=jnp.int32)
    own_lists = lax.dynamic_slice_in_dim(neighbours, first_block, own_blocks, 0)
    is_earlier = own_lists < own_ids[:, None]
    valid = is_earlier.astype(jnp.float32)
    whiten = whitening + jnp.eye(block_size, dtype=jnp.float32)[None]

    def selector(count):
        inside = (own_lists >= 0) & (own_lists < count) & is_earlier
        matches = own_lists[:, :, None] == jnp.arange(count, dtype=jnp.int32)[None, None, :]
        return (matches & inside[:, :, None]).astype(jnp.float32)

    def precondition(field):
        piece = lax.all_gather(field, ("row", "col"), axis=0, tiled=True)
        picks = selector(piece.shape[0])
        near = jnp.einsum("bkm,mcj->bkcj", picks, piece, precision=highest)
        lowered = field - jnp.einsum("bkcj,bkij->bci", near, cross, precision=highest)
        mapped = jnp.einsum("bcj,bij->bci", lowered, whiten, precision=highest)
        scaled = jnp.einsum("bci,bij->bcj", mapped, whiten, precision=highest)
        spread = (
            jnp.einsum("bci,bkij->bkcj", scaled, cross, precision=highest) * valid[:, :, None, None]
        )
        picks = selector(own_blocks * lax.axis_size(("row", "col")))
        back = lax.psum_scatter(
            jnp.einsum("bkm,bkcj->mcj", picks, spread, precision=highest),
            ("row", "col"),
            scatter_dimension=0,
            tiled=True,
        )
        return scaled - back

    own_points = lax.dynamic_slice_in_dim(points, first_block, own_blocks, 1).reshape(
        3, own_blocks * block_size
    )
    start_sum = jnp.zeros((rhs_count, own_blocks * block_size), jnp.float32)
    piece = lax.all_gather(direction, ("row", "col"), axis=0, tiled=True)
    span = piece.shape[0]
    group = math.gcd(span, 16)

    def one_group(index, running):
        begin = (index * group).astype(jnp.int32)
        column_points = lax.dynamic_slice_in_dim(points, begin, group, 1).reshape(
            3, group * block_size
        )
        column_field = (
            lax.dynamic_slice_in_dim(piece, begin, group, 0)
            .transpose(1, 0, 2)
            .reshape(rhs_count, group * block_size)
        )
        tile = covariance(own_points, column_points)
        return running + lax.dot_general(
            column_field, tile, (((1,), (1,)), ((), ())), precision=highest
        )

    image_flat = lax.fori_loop(0, span // group, one_group, start_sum)
    image = (
        image_flat.reshape(rhs_count, own_blocks, block_size).transpose(1, 0, 2)
        + nugget * direction
    )
    pre = precondition(residual)
    old, curvature = lax.psum(
        (jnp.sum(residual * pre, axis=(0, 2)), jnp.sum(direction * image, axis=(0, 2))),
        ("row", "col"),
    )
    step_size = (old / curvature)[None, :, None]
    solution_next = solution + step_size * direction
    residual_next = residual - step_size * image
    pre_next = precondition(residual_next)
    newer = lax.psum(jnp.sum(residual_next * pre_next, axis=(0, 2)), ("row", "col"))
    ratio = (newer / old)[None, :, None]
    direction_next = pre_next + ratio * direction
    return (solution_next, residual_next, direction_next)


def solution(mesh):
    placed = (
        P(),
        P(),
        P(),
        P(("row", "col"), None, None, None),
        P(("row", "col"), None, None),
        P(("row", "col"), None, None),
        P(("row", "col"), None, None),
        P(("row", "col"), None, None),
    )
    return jax.shard_map(
        per_device,
        mesh=mesh,
        in_specs=placed,
        out_specs=(
            P(("row", "col"), None, None),
            P(("row", "col"), None, None),
            P(("row", "col"), None, None),
        ),
        check_vma=False,
    )
```

profile of v0, /device:TPU:1, one launch (start us, length us, event | category | flops | bytes accessed | tf_op | source)
XLA Modules:
  0.0 1771.8 jit_solution(8504843684024733289)
XLA Ops:
  9.8 16.2 copy.23
  26.1 226.5 %gather_fusion = f32[65536,3]{1,0:T(8,128)} fusion(f32[3,65536]{0,1:T(8,128)} %copy.23, s32[65536]{0:T(1024)S(1)} %fusion.45), kind=kCustom, calls=%fused_computation | custom fusion | bytes 1835008 | tf_op jit(solution)/shard_map/gather | solution.py:27
  252.6 19.6 %copy.25 = f32[3,256,256]{2,1,0:T(8,128)} copy(f32[3,256,256]{0,2,1:T(8,128)} %bitcast.94) | data formatting | bytes 1572864
  273.3 2.9 fusion.33
  276.2 1.8 fusion.36
  280.1 1.1 convolution_bitcast_fusion.1
  281.2 2.6 copy.22
  284.0 223.9 %while.14 = (s32[]{:T(128)}, f32[8,512]{1,0:T(8,128)S(1)}, f32[256,8,256]{2,1,0:T(8,128)}, f32[3,512]{1,0:T(4,128)S(1)}, f32[3,256,256]{2,1,0:T(8,128)}, /*index...) while((s32[]{:T(128)}, f32[8,512]{1,0:T(8,128)S(1)}, ...), condition=%wide.region_4.0_spmd.clone, body=%wide.region_3.0_spmd.clone.sunk | while | flops 228597760 | bytes 690381 | solution.py:83
  285.8 12.2 fusion.88
  299.8 12.2 fusion.88
  313.8 12.2 fusion.88
  327.8 12.2 fusion.88
  341.8 12.2 fusion.88
  355.8 12.2 fusion.88
  369.8 12.2 fusion.88
  383.8 12.2 fusion.88
  397.8 12.2 fusion.88
  411.8 12.2 fusion.88
  425.8 12.2 fusion.88
  439.7 12.2 fusion.88
  453.7 12.2 fusion.88
  467.7 12.2 fusion.88
  481.7 12.2 fusion.88
  495.7 12.2 fusion.88
  508.1 412.1 %reduce-scatter.3.cloned.1.call-done = f32[2,8,256]{2,1,0:T(8,128)} async-done(((f32[256,8,256]{2,1,0:T(8,128)}), f32[2,8,256]{2,1,0:T(8,128)}) %reduce-scatter.3.cloned.1.call-update) | async-done | bytes 16400 | tf_op jit(solution)/shard_map/reduce_scatter | solution.py:52
  921.0 69.2 %all-reduce = (f32[8]{0:T(128)S(1)}, f32[8]{0:T(128)S(1)}) all-reduce(f32[8]{0:T(128)S(1)} %multiply_reduce_fusion.2, f32[8]{0:T(128)S(1)} %get-tuple-element.140), channel_id=1, replica_groups=mesh['row'=4,'col'=32] {'row','col'}, use_global_device_ids=true, to_apply=%region_2.0 | all-reduce | flops 16 | bytes 128 | tf_op jit(solution)/shard_map/psum | solution.py:89
  991.2 62.0 %all-gather.8.cloned.1.call-done = f32[256,8,256]{2,1,0:T(8,128)} async-done(((f32[2,8,256]{2,1,0:T(8,128)}), f32[256,8,256]{2,1,0:T(8,128)}) %all-gather.8.cloned.1.call-update) | async-done | bytes 2097168 | tf_op jit(solution)/shard_map/all_gather | solution.py:42
  1053.1 2.9 fusion.31
  1056.0 2.5 fusion.35
  1061.7 2.6 copy.26
  1064.3 630.2 %reduce-scatter.5.cloned.1.call-done = f32[2,8,256]{2,1,0:T(8,128)} async-done(((f32[256,8,256]{2,1,0:T(8,128)}), f32[2,8,256]{2,1,0:T(8,128)}) %reduce-scatter.5.cloned.1.call-update) | async-done | bytes 16400 | tf_op jit(solution)/shard_map/reduce_scatter | solution.py:52
  1695.3 69.2 %psum.23 = f32[8]{0:T(128)S(1)} all-reduce(f32[8]{0:T(128)S(1)} %get-tuple-element.138), channel_id=1, replica_groups=mesh['row'=4,'col'=32] {'row','col'}, use_global_device_ids=true, to_apply=%region_9.0 | all-reduce | flops 8 | bytes 64 | tf_op jit(solution)/shard_map/psum | solution.py:97
  (147 shorter events, 40.6 us)
Async XLA Ops:
  7.2 269.0 %copy-start = (f32[2,4,256,256]{3,2,1,0:T(8,128)S(1)}, f32[2,4,256,256]{3,2,1,0:T(8,128)}, u32[]{:S(2)}) copy-start(f32[2,4,256,256]{3,2,1,0:T(8,128)} %param.13) | copy-start | bytes 6291460
  7.2 266.1 %all-gather.4.cloned.1.call-start = ((), (), s32[]{:S(2)}) async-start(), calls=%async_computation.2 | async-start | bytes 2113536 | tf_op jit(solution)/shard_map/all_gather | solution.py:42
  7.9 276.1 %all-gather.6.cloned.1.call-start = ((), (), s32[]{:S(2)}) async-start(), calls=%async_computation.4 | async-start | bytes 2113536 | tf_op jit(solution)/shard_map/all_gather | solution.py:64
  8.7 911.5 %reduce-scatter.3.cloned.1.call-start = ((), (), s32[]{:S(2)}) async-start(), calls=%async_computation.3 | async-start | bytes 2113536 | tf_op jit(solution)/shard_map/reduce_scatter | solution.py:52
  9.8 16.2 copy-start.4
  252.6 23.6 %copy-start.2 = (f32[2,8,256]{2,1,0:T(8,128)S(1)}, f32[2,8,256]{2,1,0:T(8,128)}, u32[]{:S(2)}) copy-start(f32[2,8,256]{2,1,0:T(8,128)} %param.16) | copy-start | bytes 49156
  252.6 25.5 %copy-start.1 = (f32[2,256,256]{2,1,0:T(8,128)S(1)}, f32[2,256,256]{2,1,0:T(8,128)}, u32[]{:S(2)}) copy-start(f32[2,256,256]{2,1,0:T(8,128)} %param.14) | copy-start | bytes 1572868
  283.8 769.4 %all-gather.8.cloned.1.call-start = ((), (), s32[]{:S(2)}) async-start(), calls=%async_computation.5 | async-start | bytes 2113536 | tf_op jit(solution)/shard_map/all_gather | solution.py:42
  284.0 224.0 %copy-start.5 = (f32[2,8,256]{2,1,0:T(8,128)S(1)}, f32[2,8,256]{2,1,0:T(8,128)}, u32[]{:S(2)}) copy-start(f32[2,8,256]{2,1,0:T(8,128)} %param.17) | copy-start | bytes 49156
  990.2 774.4 %copy-start.6 = (f32[2,8,256]{2,1,0:T(8,128)S(1)}, f32[2,8,256]{2,1,0:T(8,128)}, u32[]{:S(2)}) copy-start(f32[2,8,256]{2,1,0:T(8,128)} %param.15) | copy-start | bytes 49156
  990.9 703.6 %copy-start.3 = (f32[2,8,256]{2,1,0:T(8,128)S(1)}, f32[2,8,256]{2,1,0:T(8,128)}, u32[]{:S(2)}) copy-start(f32[2,8,256]{2,1,0:T(8,128)} %multiply_subtract_fusion) | copy-start | bytes 49156
  990.9 703.6 %reduce-scatter.5.cloned.1.call-start = ((), (), s32[]{:S(2)}) async-start(), calls=%async_computation.6 | async-start | bytes 2113536 | tf_op jit(solution)/shard_map/reduce_scatter | solution.py:52
Sparse Core Ops, SparseCore 0:
  11.2 68.9 all-gather.3
  83.3 62.7 all-gather.5
  283.9 636.2 reduce-scatter.2
  991.0 62.0 all-gather.7
  1064.4 630.0 reduce-scatter.4
where the time goes:
time: 1780 us; the launch traced here: 1770 us
  waiting for transfers between devices  1110 us (62%)
  local copies, waits for them, and re-layouts  297 us (17%)
  matrix products  212 us (12%)
  blocking collectives  138 us (8%)
    reduce_scatter x2, waiting for transfers between devices, precondition(): lax.psum_scatter(jnp.einsum('bkm,bkcj->mcj', picks, spread, precision=hig...  1040 us
    gather x1, local copies, waits for them, and re-layouts, per_device(): points = coordinates[:, ordering].reshape(3, total_blocks, block_size)  226 us
    dot_general x16, matrix products, one_group(): lax.dot_general(column_field, tile, (((1,), (1,)), ((), ())), precision=h...  195 us
    psum x1, blocking collectives, per_device(): lax.psum(jnp.sum(residual_next * pre_next, axis=(0, 2)), ('row', 'col'))  69.2 us
    psum x1, blocking collectives, per_device(): lax.psum((jnp.sum(residual * pre, axis=(0, 2)), jnp.sum(direction * image...  69.2 us
    all_gather x2, waiting for transfers between devices, precondition(): piece = lax.all_gather(field, ('row', 'col'), axis=0, tiled=True)  62 us
    unnamed x16, local copies, waits for them, and re-layouts  35.9 us
  transfers between devices with their start and end apart: 5, of which 3 were waited for; matrix products, arithmetic and copies ran while one was open for 28% of the time, Pallas kernels for 0%

commit v1 on v0

--- a/solution.py
+++ b/solution.py
@@ -8,6 +8,11 @@
 variance = 0.05
 nugget = 1.0
 highest = lax.Precision.HIGHEST
+
+
+def axis_by_axis(value, inner_axis, outer_axis):
+    inner = lax.psum(value, inner_axis)
+    return lax.psum(inner, outer_axis)
 
 
 def covariance(rows, columns):
@@ -86,9 +91,10 @@
         + nugget * direction
     )
     pre = precondition(residual)
-    old, curvature = lax.psum(
+    old, curvature = axis_by_axis(
         (jnp.sum(residual * pre, axis=(0, 2)), jnp.sum(direction * image, axis=(0, 2))),
-        ("row", "col"),
+        "row",
+        "col",
     )
     step_size = (old / curvature)[None, :, None]
     solution_next = solution + step_size * direction

time: 1780 us -> 1780 us (level)
    psum x1 -> x2, blocking collectives: 69.2 us -> 77.3 us  [the longest x1 71.1 us: axis_by_axis(): return lax.psum(inner, outer_axis)]
where the time goes in v1:
time: 1780 us
  waiting for transfers between devices  1100 us (62%)
  local copies, waits for them, and re-layouts  296 us (17%)
  matrix products  212 us (12%)
  blocking collectives  146 us (8%)
    reduce_scatter x2, waiting for transfers between devices, precondition(): lax.psum_scatter(jnp.einsum('bkm,bkcj->mcj', picks, spread, precision=hig...  1040 us
    gather x1, local copies, waits for them, and re-layouts, per_device(): points = coordinates[:, ordering].reshape(3, total_blocks, block_size)  226 us
    dot_general x16, matrix products, one_group(): lax.dot_general(column_field, tile, (((1,), (1,)), ((), ())), precision=h...  195 us
    psum x1, blocking collectives, axis_by_axis(): return lax.psum(inner, outer_axis)  71.1 us
    psum x1, blocking collectives, per_device(): lax.psum(jnp.sum(residual_next * pre_next, axis=(0, 2)), ('row', 'col'))  69.2 us
    all_gather x2, waiting for transfers between devices, precondition(): piece = lax.all_gather(field, ('row', 'col'), axis=0, tiled=True)  60.9 us
    unnamed x16, local copies, waits for them, and re-layouts  35.9 us
  transfers between devices with their start and end apart: 5, of which 3 were waited for; matrix products, arithmetic and copies ran while one was open for 28% of the time, Pallas kernels for 0%

profile of v1, /device:TPU:1, one launch (start us, length us, event | category | flops | bytes accessed | tf_op | source)
XLA Modules:
  0.0 1778.7 jit_solution(12413722950996858092)
XLA Ops:
  9.8 16.2 copy.23
  26.1 226.1 %gather_fusion = f32[65536,3]{1,0:T(8,128)} fusion(f32[3,65536]{0,1:T(8,128)} %copy.23, s32[65536]{0:T(1024)S(1)} %fusion.45), kind=kCustom, calls=%fused_computation | custom fusion | bytes 1835008 | tf_op jit(solution)/shard_map/gather | solution.py:32
  252.2 19.6 %copy.25 = f32[3,256,256]{2,1,0:T(8,128)} copy(f32[3,256,256]{0,2,1:T(8,128)} %bitcast.94) | data formatting | bytes 1572864
  273.0 2.9 fusion.33
  275.9 1.8 fusion.36
  280.8 2.6 copy.22
  283.7 223.9 %while.14 = (s32[]{:T(128)}, f32[8,512]{1,0:T(8,128)S(1)}, f32[256,8,256]{2,1,0:T(8,128)}, f32[3,512]{1,0:T(4,128)S(1)}, f32[3,256,256]{2,1,0:T(8,128)}, /*index...) while((s32[]{:T(128)}, f32[8,512]{1,0:T(8,128)S(1)}, ...), condition=%wide.region_5.0_spmd.clone, body=%wide.region_4.0_spmd.clone.sunk | while | flops 228597760 | bytes 690381 | solution.py:88
  285.5 12.2 fusion.88
  299.5 12.2 fusion.88
  313.4 12.2 fusion.88
  327.4 12.2 fusion.88
  341.4 12.2 fusion.88
  355.4 12.2 fusion.88
  369.4 12.2 fusion.88
  383.4 12.2 fusion.88
  397.4 12.2 fusion.88
  411.4 12.2 fusion.88
  425.4 12.2 fusion.88
  439.4 12.2 fusion.88
  453.4 12.2 fusion.88
  467.4 12.2 fusion.88
  481.4 12.2 fusion.88
  495.4 12.2 fusion.88
  507.8 412.3 %reduce-scatter.3.cloned.1.call-done = f32[2,8,256]{2,1,0:T(8,128)} async-done(((f32[256,8,256]{2,1,0:T(8,128)}), f32[2,8,256]{2,1,0:T(8,128)}) %reduce-scatter.3.cloned.1.call-update) | async-done | bytes 16400 | tf_op jit(solution)/shard_map/reduce_scatter | solution.py:57
  920.9 6.1 all-reduce.1
  927.1 71.1 %all-reduce = (f32[8]{0:T(128)S(1)}, f32[8]{0:T(128)S(1)}) all-reduce(f32[8]{0:T(128)S(1)} %get-tuple-element.138, f32[8]{0:T(128)S(1)} %get-tuple-element.139), channel_id=1, replica_groups=mesh['row'=4,'col'=32] {'col'}, use_global_device_ids=true, to_apply=%region_3.0 | all-reduce | flops 16 | bytes 128 | tf_op jit(solution)/shard_map/psum | solution.py:15
  999.2 60.8 %all-gather.8.cloned.1.call-done = f32[256,8,256]{2,1,0:T(8,128)} async-done(((f32[2,8,256]{2,1,0:T(8,128)}), f32[256,8,256]{2,1,0:T(8,128)}) %all-gather.8.cloned.1.call-update) | async-done | bytes 2097168 | tf_op jit(solution)/shard_map/all_gather | solution.py:47
  1060.0 2.9 fusion.31
  1062.9 2.5 fusion.35
  1068.6 2.6 copy.26
  1071.2 630.2 %reduce-scatter.5.cloned.1.call-done = f32[2,8,256]{2,1,0:T(8,128)} async-done(((f32[256,8,256]{2,1,0:T(8,128)}), f32[2,8,256]{2,1,0:T(8,128)}) %reduce-scatter.5.cloned.1.call-update) | async-done | bytes 16400 | tf_op jit(solution)/shard_map/reduce_scatter | solution.py:57
  1702.3 69.2 %psum.39 = f32[8]{0:T(128)S(1)} all-reduce(f32[8]{0:T(128)S(1)} %get-tuple-element.140), channel_id=1, replica_groups=mesh['row'=4,'col'=32] {'row','col'}, use_global_device_ids=true, to_apply=%region_11.0 | all-reduce | flops 8 | bytes 64 | tf_op jit(solution)/shard_map/psum | solution.py:103
  (148 shorter events, 41.7 us)
Async XLA Ops:
  7.2 268.7 %copy-start = (f32[2,4,256,256]{3,2,1,0:T(8,128)S(1)}, f32[2,4,256,256]{3,2,1,0:T(8,128)}, u32[]{:S(2)}) copy-start(f32[2,4,256,256]{3,2,1,0:T(8,128)} %param.13) | copy-start | bytes 6291460
  7.2 265.8 %all-gather.4.cloned.1.call-start = ((), (), s32[]{:S(2)}) async-start(), calls=%async_computation.2 | async-start | bytes 2113536 | tf_op jit(solution)/shard_map/all_gather | solution.py:47
  7.9 275.7 %all-gather.6.cloned.1.call-start = ((), (), s32[]{:S(2)}) async-start(), calls=%async_computation.4 | async-start | bytes 2113536 | tf_op jit(solution)/shard_map/all_gather | solution.py:69
  8.7 911.4 %reduce-scatter.3.cloned.1.call-start = ((), (), s32[]{:S(2)}) async-start(), calls=%async_computation.3 | async-start | bytes 2113536 | tf_op jit(solution)/shard_map/reduce_scatter | solution.py:57
  9.8 16.2 copy-start.4
  252.2 23.6 %copy-start.2 = (f32[2,8,256]{2,1,0:T(8,128)S(1)}, f32[2,8,256]{2,1,0:T(8,128)}, u32[]{:S(2)}) copy-start(f32[2,8,256]{2,1,0:T(8,128)} %param.16) | copy-start | bytes 49156
  252.2 25.5 %copy-start.1 = (f32[2,256,256]{2,1,0:T(8,128)S(1)}, f32[2,256,256]{2,1,0:T(8,128)}, u32[]{:S(2)}) copy-start(f32[2,256,256]{2,1,0:T(8,128)} %param.14) | copy-start | bytes 1572868
  283.4 776.6 %all-gather.8.cloned.1.call-start = ((), (), s32[]{:S(2)}) async-start(), calls=%async_computation.5 | async-start | bytes 2113536 | tf_op jit(solution)/shard_map/all_gather | solution.py:47
  283.7 224.0 %copy-start.5 = (f32[2,8,256]{2,1,0:T(8,128)S(1)}, f32[2,8,256]{2,1,0:T(8,128)}, u32[]{:S(2)}) copy-start(f32[2,8,256]{2,1,0:T(8,128)} %param.17) | copy-start | bytes 49156
  998.2 773.3 %copy-start.6 = (f32[2,8,256]{2,1,0:T(8,128)S(1)}, f32[2,8,256]{2,1,0:T(8,128)}, u32[]{:S(2)}) copy-start(f32[2,8,256]{2,1,0:T(8,128)} %param.15) | copy-start | bytes 49156
  998.9 702.5 %copy-start.3 = (f32[2,8,256]{2,1,0:T(8,128)S(1)}, f32[2,8,256]{2,1,0:T(8,128)}, u32[]{:S(2)}) copy-start(f32[2,8,256]{2,1,0:T(8,128)} %multiply_subtract_fusion) | copy-start | bytes 49156
  998.9 702.5 %reduce-scatter.5.cloned.1.call-start = ((), (), s32[]{:S(2)}) async-start(), calls=%async_computation.6 | async-start | bytes 2113536 | tf_op jit(solution)/shard_map/reduce_scatter | solution.py:57
Sparse Core Ops, SparseCore 0:
  11.2 68.9 all-gather.3
  83.3 62.7 all-gather.5
  283.5 636.5 reduce-scatter.2
  999.0 60.9 all-gather.7
  1071.3 630.0 reduce-scatter.4
